TPU v7x, 32 devices: a whole 2x2x4 slice. The times are simulated.
32 devices in a mesh: ctx: 8 (over z, y), head: 4 (over x, core).
Axes of the slice: x: 2, y: 2, z: 4, core: 2. Of those that a mesh axis runs over, the one named last changes fastest.
Arguments:
- tokens: bfloat16 [4096, 1024], P('ctx'), may hold values from -24 to 24
- w_query: bfloat16 [1024, 1024], P(None, 'head'), may hold values from -0.1875 to 0.1875
- w_key: bfloat16 [1024, 1024], P(None, 'head'), may hold values from -0.1875 to 0.1875
- w_value: bfloat16 [1024, 1024], P(None, 'head'), may hold values from -0.1875 to 0.1875
- w_out: bfloat16 [1024, 1024], P('head'), may hold values from -0.1875 to 0.1875
- block_mask: int32 [32, 32], replicated, may hold values from 0 to 1, as said below
- block_order: int32 [32], replicated, may hold values from 0 to 31, each once
Outputs:
- mixed: bfloat16 [4096, 1024], P('ctx', 'head')
Inputs may be any that keep to these rules, and one draw needn't show every extreme that they name: `block_mask`: entries are 0 or 1 and every diagonal entry is 1. `block_order`: each initial block index appears once.
All inputs are finite; a program needn't handle non-finite values.
Results may differ from a plain program's by a relative error of at most 0.013.
Values may be sent and summed in bfloat16 or wider, within the bound.
No kernel may reach another device: no remote copies, remote signals or barrier semaphores. Data moves between devices by JAX's collectives and lax.ppermute only.
A program may use at most 256 MiB of HBM per device.

v0:
```python
import functools

import jax
import jax.numpy as jnp
from jax import lax
from jax.experimental import pallas as pl
from jax.experimental.pallas import tpu as pltpu
from jax.sharding import PartitionSpec as P


HEAD_DIM = 64
BLOCK = 128
LANES = 128
SLOTS = 4
STREAMS = 4
NEG = -1e30


HBM = pl.BlockSpec(memory_space=pltpu.HBM)
VMEM = pl.BlockSpec(memory_space=pltpu.VMEM)
SMEM = pl.BlockSpec(memory_space=pltpu.SMEM)
GRANT = 16 * 1024 * 1024
WHOLE = 60 * 1024 * 1024


def low_half(shape):
    return lax.broadcasted_iota(jnp.int32, shape, len(shape) - 1) < HEAD_DIM


def swap_halves(x):
    return pltpu.roll(x, HEAD_DIM, 1)


def proj_kernel(inner, far, tok_in, wk_in, wv_in, wq_in, out0, out1, tok, w, msg, sems):
    a = lax.axis_index("ctx") // inner
    group = (a // 2) ^ far
    cols = pl.ds(pl.multiple_of(group * LANES, LANES), LANES)
    loads = [pltpu.make_async_copy(tok_in, tok, sems.at[0])] + [
        pltpu.make_async_copy(src.at[:, cols], w.at[:, pl.ds(n * LANES, LANES)], sems.at[n + 1])
        for n, src in enumerate((wv_in, wq_in, wk_in))
    ]
    for load in loads:
        load.start()
    rows = tok.shape[0]
    half = rows // 2
    low = low_half((half, LANES))
    for load in loads:
        load.wait()
    vqk = jnp.dot(tok[...], w[...], preferred_element_type=jnp.float32)
    v, q, k = (vqk[:, n * LANES : (n + 1) * LANES] for n in range(3))
    q = q * HEAD_DIM ** (-0.5)
    for base, x in ((half, v), (rows, q)):
        for i in range(rows // BLOCK):
            turned = jnp.transpose(x[i * BLOCK : (i + 1) * BLOCK]).astype(jnp.bfloat16)
            start = base + i * HEAD_DIM
            msg[0, start : start + HEAD_DIM] = turned[:HEAD_DIM]
            msg[1, start : start + HEAD_DIM] = turned[HEAD_DIM:]
    top, bottom = k[:half], k[half:]
    msg[0, :half] = jnp.where(low, top, swap_halves(bottom)).astype(jnp.bfloat16)
    msg[1, :half] = jnp.where(low, swap_halves(top), bottom).astype(jnp.bfloat16)
    odd = lax.rem(a, 2)
    out0[...] = msg[odd]
    out1[...] = msg[1 - odd]


def list_kernel(inner, outer, per, cap, mask, order, who, where, which, valid, first, steps, names, ends, load):
    c = lax.axis_index("ctx")
    a = c // inner
    b = (c % inner) // 2 * 2 + lax.axis_index("head") % 2
    blocks = inner * outer * per
    half = per // 2
    span = blocks + SLOTS

    def name(dev, _):
        kb = ((lax.div(dev, inner) ^ a) * inner + (lax.rem(dev, inner) ^ b)) * per
        for i in range(per):
            names[dev * per + i] = order[kb + i // 2 + i % 2 * half]
        return 0

    lax.fori_loop(0, inner * outer, name, 0)

    def piece(k, _):
        qb = ((k ^ a) * inner + b) * per
        own = [order[qb + i] for i in range(per)]

        def col(n, to):
            to = list(to)
            for e in range(8):
                slot = n * 8 + e
                key = names[slot]
                for i in range(per):
                    which[to[i]] = slot
                    to[i] = to[i] + mask[own[i], key]
            return tuple(to)

        begin = [(k * per + i) * span for i in range(per)]
        end = lax.fori_loop(0, blocks // 8, col, tuple(begin))
        for i in range(per):
            keep = which[begin[i]]
            for extra in range(SLOTS):
                which[end[i] + extra] = keep
            ends[k * per + i] = end[i]
        return 0

    lax.fori_loop(0, outer, piece, 0)
    for s in range(STREAMS):
        load[s] = 0

    def row(qi, _):
        s, least = jnp.int32(0), load[0]
        for other in range(1, STREAMS):
            here = load[other]
            s = jnp.where(here < least, other, s)
            least = jnp.minimum(here, least)
        item = s * cap + least
        start = qi * span
        count = ends[qi] - start
        items = lax.div(count + (SLOTS - 1), SLOTS)

        def mark(t, left):
            who[item + t] = qi
            where[item + t] = start + t * SLOTS
            valid[item + t] = left
            first[item + t] = 0
            return left - SLOTS

        lax.fori_loop(0, items, mark, count)
        first[item] = 1
        load[s] = least + items
        return 0

    lax.fori_loop(0, outer * per, row, 0)
    most = load[0]
    for s in range(1, STREAMS):
        most = jnp.maximum(most, load[s])
    steps[0] = most
    for s in range(STREAMS):
        start = s * cap
        last = start + jnp.maximum(load[s] - 1, 0)
        idle = load[s] == 0
        qi = jnp.where(idle, outer * per, who[last])
        key = jnp.where(idle, 0, where[last])

        def fill(t, _):
            who[start + t] = qi
            where[start + t] = key
            valid[start + t] = 0
            first[start + t] = 0
            return 0

        lax.fori_loop(load[s], most + 2, fill, 0)


def attend_kernel(per, cap, n_kv, start_q, n_q, who, where, which, valid, first, steps, *rest):
    ins, rest = rest[:n_kv], rest[n_kv:]
    q_in = ins[:: n_kv // n_q]
    outs, rest = rest[:n_q], rest[n_q:]
    kq, vt, qt, sc, m_s, al_s, l_s, acc_s, l_all, acc_all = rest
    half = per // 2
    nq = n_q * per
    zero = jnp.zeros((HEAD_DIM, BLOCK), jnp.bfloat16)
    for k, msg in enumerate(q_in):
        for i in range(per):
            turned = msg[start_q + i * HEAD_DIM : start_q + (i + 1) * HEAD_DIM, :]
            qt[0, k * per + i] = jnp.concatenate([turned, zero], axis=0)
            qt[1, k * per + i] = jnp.concatenate([zero, turned], axis=0)
    qt[:, nq] = jnp.zeros((2, LANES, BLOCK), jnp.bfloat16)
    for n, msg in enumerate(ins):
        for r in range(half):
            kq[n * half + r] = msg[r * BLOCK : (r + 1) * BLOCK, :]
        for i in range(per):
            start = half * BLOCK + (i // 2 + i % 2 * half) * HEAD_DIM
            vt[n * per + i] = msg[start : start + HEAD_DIM, :]
    m_s[...] = jnp.full(m_s.shape, NEG, jnp.float32)
    l_s[...] = jnp.zeros(l_s.shape, jnp.float32)
    acc_s[...] = jnp.zeros(acc_s.shape, jnp.float32)

    def keys(s, t):
        start = where[s * cap + t]
        return [which[start + e] for e in range(SLOTS)]

    def score(t, buf):
        for s in range(STREAMS):
            qi = who[s * cap + t]
            tiles = []
            for e, slot in enumerate(keys(s, t)):
                tile = jnp.dot(
                    kq[slot >> 1], qt[slot & 1, qi], preferred_element_type=jnp.float32
                )
                sc[buf, s, e] = tile
                tiles.append(tile.reshape(BLOCK // 8, 8, BLOCK))
            top = jnp.max(functools.reduce(jnp.maximum, tiles), axis=0)
            top = jnp.max(top, axis=0, keepdims=True)
            m_old = jnp.where(first[s * cap + t] == 1, NEG, m_s[1 - buf, s])
            m_new = jnp.maximum(m_old, top)
            al_s[buf, s] = jnp.exp(m_old - m_new)
            m_s[buf, s] = m_new

    def weigh(t, buf):
        for s in range(STREAMS):
            qi = who[s * cap + t]
            n_valid = valid[s * cap + t]
            m, alpha = m_s[buf, s], al_s[buf, s]
            acc = acc_s[s] * alpha
            total = l_s[s] * alpha
            ids = keys(s, t)
            for e in range(0, SLOTS, 2):
                probs = []
                for f in (e, e + 1):
                    shut = m + jnp.where(f < n_valid, 0.0, -NEG)
                    p = jnp.exp(sc[buf, s, f] - shut)
                    total = total + jnp.sum(p.reshape(BLOCK // 8, 8, BLOCK), axis=0)
                    probs.append(p.astype(jnp.bfloat16))
                acc = acc + jnp.dot(
                    jnp.concatenate([vt[ids[e]], vt[ids[e + 1]]], axis=1),
                    jnp.concatenate(probs, axis=0),
                    preferred_element_type=jnp.float32,
                )
            acc_s[s] = acc
            l_s[s] = total
            acc_all[qi] = acc
            l_all[qi] = total

    score(0, 0)
    count = steps[0]

    def step(u, _):
        t = 2 * u
        score(t + 1, 1)
        weigh(t, 0)
        score(t + 2, 0)
        weigh(t + 1, 1)
        return 0

    lax.fori_loop(0, lax.div(count, 2), step, 0)

    @pl.when(lax.rem(count, 2) == 1)
    def _():
        weigh(count - 1, 0)

    for k in range(n_q):
        for r in range(half):
            done = []
            for i in (k * per + r, k * per + r + half):
                done.append(acc_all[i] * (1.0 / jnp.sum(l_all[i], axis=0, keepdims=True)))
            outs[k][r * BLOCK : (r + 1) * BLOCK, :] = jnp.transpose(
                jnp.concatenate(done, axis=0)
            ).astype(jnp.bfloat16)


def out_kernel(inner, heads, groups, other, *refs):
    pieces = [refs[g * heads : (g + 1) * heads] for g in range(groups)]
    ws = refs[groups * heads : groups * heads + groups]
    out = refs[-1]
    a = lax.axis_index("ctx") // inner
    side = (lax.axis_index("head") % 2) ^ other
    cols = pl.ds(pl.multiple_of(side * out.shape[1], LANES), out.shape[1])
    half = pieces[0][0].shape[0]
    low = low_half((half, LANES))
    tops, bottoms, rows = [], [], []
    for g in range(groups):
        for k in range(0, heads, 2):
            p0 = pieces[g][k][...].astype(jnp.float32)
            p1 = pieces[g][k + 1][...].astype(jnp.float32)
            tops.append(jnp.where(low, p0, swap_halves(p1)).astype(jnp.bfloat16))
            bottoms.append(jnp.where(low, swap_halves(p0), p1).astype(jnp.bfloat16))
            for e in (0, 1):
                start = pl.multiple_of(HEAD_DIM * (a ^ (k + e)), HEAD_DIM)
                rows.append(ws[g][pl.ds(start, HEAD_DIM), cols])
    w = jnp.concatenate(rows, axis=0)
    for n, parts in enumerate((tops, bottoms)):
        x = jnp.concatenate(parts, axis=1)
        total = jnp.dot(x, w, preferred_element_type=jnp.float32)
        if not other:
            total = total + refs[-2][n * half : (n + 1) * half, :].astype(jnp.float32)
        out[n * half : (n + 1) * half, :] = total.astype(out.dtype)


def solution(mesh):
    ctx, groups = mesh.shape["ctx"], mesh.shape["head"]

    def body(tokens, w_query, w_key, w_value, w_out, block_mask, block_order):
        rows = tokens.shape[0]
        heads = w_query.shape[1] // HEAD_DIM
        inner = ctx // heads
        per = rows // BLOCK
        nb = block_mask.shape[0]
        nq = heads * per
        cols = w_out.shape[1] // groups
        bf = jnp.bfloat16
        params = pltpu.CompilerParams(vmem_limit_bytes=GRANT)
        both = ("ctx", "head")
        places = [(c // inner, c % inner, h) for c in range(ctx) for h in range(groups)]

        def index(a, b, h):
            return (a * inner + b) * groups + h

        def turn(x, j):
            pairs = [
                (index(a, b, h), index(a ^ j, (b & ~1) | (h & 1), (h & ~1) | (b & 1)))
                for a, b, h in places
            ]
            return lax.ppermute(x, both, pairs)

        def spread(x, e):
            pairs = [
                (index(a, b, h), index(a, b ^ (e & ~1), h ^ (e & 1))) for a, b, h in places
            ]
            return lax.ppermute(x, both, pairs) if e else x

        def head_swap(x, j):
            return lax.ppermute(x, "head", [(h, h ^ j) for h in range(groups)]) if j else x

        half, size = rows // 2, rows + rows // 2
        msgs = []
        for far in range(heads // 2):
            msgs += pl.pallas_call(
                functools.partial(proj_kernel, inner, far),
                out_shape=[jax.ShapeDtypeStruct((size, LANES), bf)] * 2,
                in_specs=[HBM] * 4,
                out_specs=[VMEM] * 2,
                scratch_shapes=[pltpu.VMEM(tokens.shape, bf)]
                + [
                    pltpu.VMEM((tokens.shape[1], 3 * LANES), bf),
                    pltpu.VMEM((2, size, LANES), bf),
                    pltpu.SemaphoreType.DMA((4,)),
                ],
                compiler_params=pltpu.CompilerParams(vmem_limit_bytes=WHOLE),
            )(tokens, w_key, w_value, w_query)
        got = [None] * heads
        for j in reversed(range(heads)):
            got[j] = turn(msgs[j], j)
        longest = -(-nb // SLOTS)
        cap = -(-nq * longest // STREAMS) + longest + 3
        table = jax.ShapeDtypeStruct((STREAMS * cap,), jnp.int32)
        tables = pl.pallas_call(
            functools.partial(list_kernel, inner, heads, per, cap),
            out_shape=[
                table,
                table,
                jax.ShapeDtypeStruct((nq * (nb + SLOTS),), jnp.int32),
                table,
                table,
                jax.ShapeDtypeStruct((1,), jnp.int32),
            ],
            in_specs=[SMEM] * 2,
            out_specs=[SMEM] * 6,
            scratch_shapes=[
                pltpu.SMEM((nb,), jnp.int32),
                pltpu.SMEM((nq,), jnp.int32),
                pltpu.SMEM((STREAMS,), jnp.int32),
            ],
            name="block_lists",
        )(block_mask, block_order)
        x = lax.axis_index("head") // 2
        w_out, msgs = lax.optimization_barrier((w_out, msgs))
        w_cols = []
        for g in range(0, groups, 2):
            share = lax.dynamic_slice_in_dim(w_out, (x ^ g // 2) * 2 * cols, 2 * cols, axis=1)
            w_cols.append(head_swap(share, g))
        got[0], tables, w_cols = lax.optimization_barrier((got[0], tables, w_cols))
        kv = []
        for j in range(heads):
            for e in range(inner):
                kv.append(spread(got[j], e))
        o = pl.pallas_call(
            functools.partial(attend_kernel, per, cap, len(kv), rows, heads),
            out_shape=[jax.ShapeDtypeStruct((half, LANES), bf)] * heads,
            in_specs=[SMEM] * 6 + [VMEM] * len(kv),
            out_specs=[VMEM] * heads,
            scratch_shapes=[
                pltpu.VMEM((nb // 2, BLOCK, LANES), bf),
                pltpu.VMEM((nb, HEAD_DIM, BLOCK), bf),
                pltpu.VMEM((2, nq + 1, LANES, BLOCK), bf),
                pltpu.VMEM((2, STREAMS, SLOTS, BLOCK, BLOCK), jnp.float32),
                pltpu.VMEM((2, STREAMS, 1, BLOCK), jnp.float32),
                pltpu.VMEM((2, STREAMS, 1, BLOCK), jnp.float32),
                pltpu.VMEM((STREAMS, 8, BLOCK), jnp.float32),
                pltpu.VMEM((STREAMS, HEAD_DIM, BLOCK), jnp.float32),
                pltpu.VMEM((nq + 1, 8, BLOCK), jnp.float32),
                pltpu.VMEM((nq + 1, HEAD_DIM, BLOCK), jnp.float32),
            ],
            compiler_params=params,
            name="attend",
        )(*tables, *kv)
        mine = [None] * heads
        for j in reversed(range(heads)):
            mine[j] = turn(o[j], j)
        pieces = []
        for g in range(0, groups, 2):
            for j in range(heads):
                pieces.append(head_swap(mine[j], g))

        def out(other, *more):
            return pl.pallas_call(
                functools.partial(out_kernel, inner, heads, groups // 2, other),
                out_shape=jax.ShapeDtypeStruct((rows, cols), bf),
                in_specs=[VMEM] * (len(pieces) + len(w_cols) + len(more)),
                out_specs=VMEM,
                compiler_params=params,
            )(*pieces, *w_cols, *more)

        return out(0, head_swap(out(1), 1))

    placed = (
        P("ctx", None),
        P(None, "head"),
        P(None, "head"),
        P(None, "head"),
        P("head", None),
        P(),
        P(),
    )
    return jax.shard_map(
        body, mesh=mesh, in_specs=placed, out_specs=P("ctx", "head"), check_vma=False
    )
```

profile of v0, /device:TPU:0, one launch (start us, length us, event | category | flops | bytes accessed | tf_op | source)
XLA Modules:
  0.0 56.6 jit_solution(16369897393211635282)
XLA Ops:
  0.0 3.1 %shard_map.74 = (bf16[768,128]{1,0:T(8,128)(2,1)}, bf16[768,128]{1,0:T(8,128)(2,1)}) custom-call(bf16[512,1024]{1,0:T(8,128)(2,1)} %tok_in.3, bf16[1024,256]{1,0:T(8,128)(2,1)} %wk_in.3, bf16[1024,256]{1,0:T(8,128)(2,1)} %wv_in.3, bf16[1024,256]{1,0:T(8,128)(2,1)} %wq_in.3), custom_call_target="tpu_custom_call" | custom-call | tf_op jit(solution)/shard_map/pallas_call | solution.py:317
  3.1 0.0 copy-start.5
  3.1 3.2 %shard_map.73 = (bf16[768,128]{1,0:T(8,128)(2,1)}, bf16[768,128]{1,0:T(8,128)(2,1)}) custom-call(bf16[512,1024]{1,0:T(8,128)(2,1)} %tok_in.3, bf16[1024,256]{1,0:T(8,128)(2,1)} %wk_in.3, bf16[1024,256]{1,0:T(8,128)(2,1)} %wv_in.3, bf16[1024,256]{1,0:T(8,128)(2,1)} %wq_in.3), custom_call_target="tpu_custom_call" | custom-call | tf_op jit(solution)/shard_map/pallas_call | solution.py:317
  6.3 0.0 copy-done.5
  6.3 0.0 copy-start.9
  6.3 0.0 copy-start.8
  6.3 0.0 copy-start.7
  6.3 0.0 copy-start.6
  6.4 3.0 %collective-permute-start.1 = (bf16[256,512]{1,0:T(8,128)(2,1)S(1)}, bf16[256,512]{1,0:T(8,128)(2,1)S(1)}, u32[]{:S(2)}, u32[]{:S(2)}) collective-permute-start(bf16[256,512]{1,0:T(8,128)(2,1)S(1)} %get-tuple-element.53), channel_id=1, source_target_pairs={{0,2},{1,3},{2,0},{3,1},{4,6},{5,7},{6,4},{7,5},{8,10},{9,11},{10,... | collective-permute-start | bytes 786440 | tf_op jit(solution)/shard_map/ppermute | solution.py:312
  9.4 0.0 copy-done.9
  9.4 2.6 %collective-permute-start.5 = (bf16[768,128]{1,0:T(8,128)(2,1)S(1)}, bf16[768,128]{1,0:T(8,128)(2,1)S(1)}, u32[]{:S(2)}, u32[]{:S(2)}) collective-permute-start(bf16[768,128]{1,0:T(8,128)(2,1)S(1)} %copy-done.9), channel_id=1, source_target_pairs={{0,16},{1,20},{2,18},{3,22},{4,17},{5,21},{6,19},{7,23},{8,24},{9,... | collective-permute-start | bytes 589832 | tf_op jit(solution)/shard_map/ppermute | solution.py:303
  12.1 0.0 copy-done.8
  12.1 1.4 %collective-permute-start.7 = (bf16[768,128]{1,0:T(8,128)(2,1)S(1)}, bf16[768,128]{1,0:T(8,128)(2,1)S(1)}, u32[]{:S(2)}, u32[]{:S(2)}) collective-permute-start(bf16[768,128]{1,0:T(8,128)(2,1)S(1)} %copy-done.8), channel_id=1, source_target_pairs={{0,24},{1,28},{2,26},{3,30},{4,25},{5,29},{6,27},{7,31},{8,16},{9,... | collective-permute-start | bytes 589832 | tf_op jit(solution)/shard_map/ppermute | solution.py:303
  13.4 0.0 copy-done.7
  13.4 0.3 collective-permute-start.3
  13.7 0.0 copy-done.6
  13.7 0.7 %collective-permute-start = (bf16[768,128]{1,0:T(8,128)(2,1)S(1)}, bf16[768,128]{1,0:T(8,128)(2,1)S(1)}, u32[]{:S(2)}, u32[]{:S(2)}) collective-permute-start(bf16[768,128]{1,0:T(8,128)(2,1)S(1)} %copy-done.6), channel_id=1, source_target_pairs={{0,0},{1,4},{2,2},{3,6},{4,1},{5,5},{6,3},{7,7},{8,8},{9,12},{10,1... | collective-permute-start | bytes 589832 | tf_op jit(solution)/shard_map/ppermute | solution.py:303
  14.4 3.7 %block_lists.1 = (s32[172]{0:T(256)}, s32[172]{0:T(256)}, s32[576]{0:T(1024)}, s32[172]{0:T(256)}, s32[172]{0:T(256)}, /*index=5*/s32[1]{0:T(128)}) custom-call(s32[32,32]{1,0:T(8,128)} %mask.1, s32[32]{0:T(128)} %order.1), custom_call_target="tpu_custom_call" | custom-call | tf_op jit(solution)/shard_map/block_lists/pallas_call | solution.py:336
  18.1 8.1 %collective-permute-done.5.rest_4_ = bf16[768,128]{1,0:T(8,128)(2,1)S(1)} collective-permute-done((bf16[768,128]{1,0:T(8,128)(2,1)S(1)}, bf16[768,128]{1,0:T(8,128)(2,1)S(1)}, u32[]{:S(2)}, u32[]{:S(2)}) %collective-permute-start.5) | collective-permute-done | bytes 196640 | tf_op jit(solution)/shard_map/ppermute | solution.py:303
  26.3 0.8 %collective-permute-start.6 = (bf16[768,128]{1,0:T(8,128)(2,1)S(1)}, bf16[768,128]{1,0:T(8,128)(2,1)S(1)}, u32[]{:S(2)}, u32[]{:S(2)}) collective-permute-start(bf16[768,128]{1,0:T(8,128)(2,1)S(1)} %collective-permute-done.5.rest_4_), channel_id=1, source_target_pairs={{0,1},{1,0},{2,3},{3,2},{4,5},{5,4},{6,7},{7,6},{8,9},{9,8},{10,11... | collective-permute-start | bytes 589832 | tf_op jit(solution)/shard_map/ppermute | solution.py:309
  27.0 0.0 collective-permute-done.7.rest_6_
  27.0 0.0 collective-permute-start.8
  27.0 0.4 collective-permute-done.3.rest_2_
  27.5 0.1 collective-permute-start.4
  27.6 0.0 collective-permute-done.rest_0_
  27.6 0.0 collective-permute-done.1.refs_9_
  27.6 0.0 copy-start.4
  27.6 0.0 copy-start
  27.6 0.0 copy-start.2
  27.6 0.0 copy-start.3
  27.6 0.0 copy-start.1
  27.6 0.5 collective-permute-start.2
  28.1 0.0 collective-permute-done.6.rest_5_
  28.1 0.4 collective-permute-done.8.rest_7_
  28.5 0.4 collective-permute-done.4.rest_3_
  28.9 0.3 collective-permute-done.2.rest_1_
  29.2 0.0 copy-done.4
  29.2 0.0 copy-done
  29.2 0.0 copy-done.2
  29.2 0.0 copy-done.3
  29.2 0.0 copy-done.1
  29.2 5.8 %attend.1 = (bf16[256,128]{1,0:T(8,128)(2,1)S(1)}, bf16[256,128]{1,0:T(8,128)(2,1)S(1)}, bf16[256,128]{1,0:T(8,128)(2,1)S(1)}, bf16[256,128]{1,0:T(8,128)(2,1)S(1)}) custom-call(s32[172]{0:T(256)S(1)} %copy-done.1, s32[172]{0:T(256)S(1)} %copy-done.2, s32[576]{0:T(1024)S(1)} %copy-done, s32[172]{0:T(256)S(1)} %copy-done.3, s32[172]{0:T(256)S(1)} %copy-done.4, ...), custom_call_target="tpu_custom_call" | custom-call | tf_op jit(solution)/shard_map/attend/pallas_call | solution.py:366
  35.0 0.7 %collective-permute-start.9 = (bf16[256,128]{1,0:T(8,128)(2,1)S(1)}, bf16[256,128]{1,0:T(8,128)(2,1)S(1)}, u32[]{:S(2)}, u32[]{:S(2)}) collective-permute-start(bf16[256,128]{1,0:T(8,128)(2,1)S(1)} %get-tuple-element.47), channel_id=1, source_target_pairs={{0,0},{1,4},{2,2},{3,6},{4,1},{5,5},{6,3},{7,7},{8,8},{9,12},{10,1... | collective-permute-start | bytes 196616 | tf_op jit(solution)/shard_map/ppermute | solution.py:303
  35.7 4.4 %collective-permute-start.10 = (bf16[256,128]{1,0:T(8,128)(2,1)S(1)}, bf16[256,128]{1,0:T(8,128)(2,1)S(1)}, u32[]{:S(2)}, u32[]{:S(2)}) collective-permute-start(bf16[256,128]{1,0:T(8,128)(2,1)S(1)} %get-tuple-element.48), channel_id=1, source_target_pairs={{0,8},{1,12},{2,10},{3,14},{4,9},{5,13},{6,11},{7,15},{8,0},{9,4},... | collective-permute-start | bytes 196616 | tf_op jit(solution)/shard_map/ppermute | solution.py:303
  40.1 2.0 %collective-permute-start.11 = (bf16[256,128]{1,0:T(8,128)(2,1)S(1)}, bf16[256,128]{1,0:T(8,128)(2,1)S(1)}, u32[]{:S(2)}, u32[]{:S(2)}) collective-permute-start(bf16[256,128]{1,0:T(8,128)(2,1)S(1)} %get-tuple-element.49), channel_id=1, source_target_pairs={{0,16},{1,20},{2,18},{3,22},{4,17},{5,21},{6,19},{7,23},{8,24},{9,... | collective-permute-start | bytes 196616 | tf_op jit(solution)/shard_map/ppermute | solution.py:303
  42.1 1.4 %collective-permute-start.12 = (bf16[256,128]{1,0:T(8,128)(2,1)S(1)}, bf16[256,128]{1,0:T(8,128)(2,1)S(1)}, u32[]{:S(2)}, u32[]{:S(2)}) collective-permute-start(bf16[256,128]{1,0:T(8,128)(2,1)S(1)} %get-tuple-element.50), channel_id=1, source_target_pairs={{0,24},{1,28},{2,26},{3,30},{4,25},{5,29},{6,27},{7,31},{8,16},{9,... | collective-permute-start | bytes 196616 | tf_op jit(solution)/shard_map/ppermute | solution.py:303
  43.5 0.0 collective-permute-done.9.refs_0_
  43.5 0.8 %collective-permute-start.13 = (bf16[256,128]{1,0:T(8,128)(2,1)S(1)}, bf16[256,128]{1,0:T(8,128)(2,1)S(1)}, u32[]{:S(2)}, u32[]{:S(2)}) collective-permute-start(bf16[256,128]{1,0:T(8,128)(2,1)S(1)} %collective-permute-done.9.refs_0_), channel_id=1, source_target_pairs={{0,2},{1,3},{2,0},{3,1},{4,6},{5,7},{6,4},{7,5},{8,10},{9,11},{10,... | collective-permute-start | bytes 196616 | tf_op jit(solution)/shard_map/ppermute | solution.py:312
  44.3 0.0 collective-permute-done.10.refs_1_
  44.3 1.2 %collective-permute-start.14 = (bf16[256,128]{1,0:T(8,128)(2,1)S(1)}, bf16[256,128]{1,0:T(8,128)(2,1)S(1)}, u32[]{:S(2)}, u32[]{:S(2)}) collective-permute-start(bf16[256,128]{1,0:T(8,128)(2,1)S(1)} %collective-permute-done.10.refs_1_), channel_id=1, source_target_pairs={{0,2},{1,3},{2,0},{3,1},{4,6},{5,7},{6,4},{7,5},{8,10},{9,11},{10,... | collective-permute-start | bytes 196616 | tf_op jit(solution)/shard_map/ppermute | solution.py:312
  45.5 0.0 collective-permute-done.11.refs_2_
  45.5 0.8 %collective-permute-start.15 = (bf16[256,128]{1,0:T(8,128)(2,1)S(1)}, bf16[256,128]{1,0:T(8,128)(2,1)S(1)}, u32[]{:S(2)}, u32[]{:S(2)}) collective-permute-start(bf16[256,128]{1,0:T(8,128)(2,1)S(1)} %collective-permute-done.11.refs_2_), channel_id=1, source_target_pairs={{0,2},{1,3},{2,0},{3,1},{4,6},{5,7},{6,4},{7,5},{8,10},{9,11},{10,... | collective-permute-start | bytes 196616 | tf_op jit(solution)/shard_map/ppermute | solution.py:312
  46.3 2.6 %collective-permute-done.12.refs_3_ = bf16[256,128]{1,0:T(8,128)(2,1)S(1)} collective-permute-done((bf16[256,128]{1,0:T(8,128)(2,1)S(1)}, bf16[256,128]{1,0:T(8,128)(2,1)S(1)}, u32[]{:S(2)}, u32[]{:S(2)}) %collective-permute-start.12) | collective-permute-done | bytes 65568 | tf_op jit(solution)/shard_map/ppermute | solution.py:303
  48.9 0.7 %collective-permute-start.16 = (bf16[256,128]{1,0:T(8,128)(2,1)S(1)}, bf16[256,128]{1,0:T(8,128)(2,1)S(1)}, u32[]{:S(2)}, u32[]{:S(2)}) collective-permute-start(bf16[256,128]{1,0:T(8,128)(2,1)S(1)} %collective-permute-done.12.refs_3_), channel_id=1, source_target_pairs={{0,2},{1,3},{2,0},{3,1},{4,6},{5,7},{6,4},{7,5},{8,10},{9,11},{10,... | collective-permute-start | bytes 196616 | tf_op jit(solution)/shard_map/ppermute | solution.py:312
  49.6 0.0 collective-permute-done.13.refs_4_
  49.6 0.0 collective-permute-done.14.refs_5_
  49.6 0.4 collective-permute-done.15.refs_6_
  50.0 3.1 %collective-permute-done.16.refs_7_ = bf16[256,128]{1,0:T(8,128)(2,1)S(1)} collective-permute-done((bf16[256,128]{1,0:T(8,128)(2,1)S(1)}, bf16[256,128]{1,0:T(8,128)(2,1)S(1)}, u32[]{:S(2)}, u32[]{:S(2)}) %collective-permute-start.16) | collective-permute-done | bytes 65568 | tf_op jit(solution)/shard_map/ppermute | solution.py:312
  53.1 0.4 shard_map.75
  53.5 0.9 %collective-permute-start.17 = (bf16[512,256]{1,0:T(8,128)(2,1)S(1)}, bf16[512,256]{1,0:T(8,128)(2,1)S(1)}, u32[]{:S(2)}, u32[]{:S(2)}) collective-permute-start(bf16[512,256]{1,0:T(8,128)(2,1)S(1)} %shard_map.75), channel_id=1, source_target_pairs={{0,1},{1,0},{2,3},{3,2},{4,5},{5,4},{6,7},{7,6},{8,9},{9,8},{10,11... | collective-permute-start | bytes 786440 | tf_op jit(solution)/shard_map/ppermute | solution.py:312
  54.4 1.2 %collective-permute-done.17.refs_10_ = bf16[512,256]{1,0:T(8,128)(2,1)S(1)} collective-permute-done((bf16[512,256]{1,0:T(8,128)(2,1)S(1)}, bf16[512,256]{1,0:T(8,128)(2,1)S(1)}, u32[]{:S(2)}, u32[]{:S(2)}) %collective-permute-start.17) | collective-permute-done | bytes 262176 | tf_op jit(solution)/shard_map/ppermute | solution.py:312
  55.5 1.1 %shard_map.76 = bf16[512,256]{1,0:T(8,128)(2,1)} custom-call(bf16[256,128]{1,0:T(8,128)(2,1)S(1)} %collective-permute-done.9.refs_0_, bf16[256,128]{1,0:T(8,128)(2,1)S(1)} %collective-permute-done.10.refs_1_, bf16[256,128]{1,0:T(8,128)(2,1)S(1)} %collective-permute-done.11.refs_2_, bf16[256,128]{1,0:T(8,128)(2,1)S(1)} %collective-permute-done.12.refs_3_, ...), custom_call_target="tpu_custom_call" | custom-call | tf_op jit(solution)/shard_map/pallas_call | solution.py:395
  (1 shorter events, 0.0 us)
Async XLA Ops:
  3.1 3.2 %copy-start.5 = (bf16[256,1024]{1,0:T(8,128)(2,1)S(1)}, bf16[256,1024]{1,0:T(8,128)(2,1)}, u32[]{:S(2)}) copy-start(bf16[256,1024]{1,0:T(8,128)(2,1)} %param.11) | copy-start | bytes 1572868
  6.3 3.1 %copy-start.9 = (bf16[768,128]{1,0:T(8,128)(2,1)S(1)}, bf16[768,128]{1,0:T(8,128)(2,1)}, u32[]{:S(2)}) copy-start(bf16[768,128]{1,0:T(8,128)(2,1)} %get-tuple-element.37) | copy-start | bytes 589828
  6.3 5.7 %copy-start.8 = (bf16[768,128]{1,0:T(8,128)(2,1)S(1)}, bf16[768,128]{1,0:T(8,128)(2,1)}, u32[]{:S(2)}) copy-start(bf16[768,128]{1,0:T(8,128)(2,1)} %get-tuple-element.38) | copy-start | bytes 589828
  6.3 7.1 %copy-start.7 = (bf16[768,128]{1,0:T(8,128)(2,1)S(1)}, bf16[768,128]{1,0:T(8,128)(2,1)}, u32[]{:S(2)}) copy-start(bf16[768,128]{1,0:T(8,128)(2,1)} %get-tuple-element.36) | copy-start | bytes 589828
  6.3 7.4 %copy-start.6 = (bf16[768,128]{1,0:T(8,128)(2,1)S(1)}, bf16[768,128]{1,0:T(8,128)(2,1)}, u32[]{:S(2)}) copy-start(bf16[768,128]{1,0:T(8,128)(2,1)} %get-tuple-element.29) | copy-start | bytes 589828
  6.4 21.2 %collective-permute-start.1 = (bf16[256,512]{1,0:T(8,128)(2,1)S(1)}, bf16[256,512]{1,0:T(8,128)(2,1)S(1)}, u32[]{:S(2)}, u32[]{:S(2)}) collective-permute-start(bf16[256,512]{1,0:T(8,128)(2,1)S(1)} %get-tuple-element.53), channel_id=1, source_target_pairs={{0,2},{1,3},{2,0},{3,1},{4,6},{5,7},{6,4},{7,5},{8,10},{9,11},{10,... | collective-permute-start | bytes 786440 | tf_op jit(solution)/shard_map/ppermute | solution.py:312
  9.4 16.8 %collective-permute-start.5 = (bf16[768,128]{1,0:T(8,128)(2,1)S(1)}, bf16[768,128]{1,0:T(8,128)(2,1)S(1)}, u32[]{:S(2)}, u32[]{:S(2)}) collective-permute-start(bf16[768,128]{1,0:T(8,128)(2,1)S(1)} %copy-done.9), channel_id=1, source_target_pairs={{0,16},{1,20},{2,18},{3,22},{4,17},{5,21},{6,19},{7,23},{8,24},{9,... | collective-permute-start | bytes 589832 | tf_op jit(solution)/shard_map/ppermute | solution.py:303
  12.1 15.0 %collective-permute-start.7 = (bf16[768,128]{1,0:T(8,128)(2,1)S(1)}, bf16[768,128]{1,0:T(8,128)(2,1)S(1)}, u32[]{:S(2)}, u32[]{:S(2)}) collective-permute-start(bf16[768,128]{1,0:T(8,128)(2,1)S(1)} %copy-done.8), channel_id=1, source_target_pairs={{0,24},{1,28},{2,26},{3,30},{4,25},{5,29},{6,27},{7,31},{8,16},{9,... | collective-permute-start | bytes 589832 | tf_op jit(solution)/shard_map/ppermute | solution.py:303
  13.4 14.1 %collective-permute-start.3 = (bf16[768,128]{1,0:T(8,128)(2,1)S(1)}, bf16[768,128]{1,0:T(8,128)(2,1)S(1)}, u32[]{:S(2)}, u32[]{:S(2)}) collective-permute-start(bf16[768,128]{1,0:T(8,128)(2,1)S(1)} %copy-done.7), channel_id=1, source_target_pairs={{0,8},{1,12},{2,10},{3,14},{4,9},{5,13},{6,11},{7,15},{8,0},{9,4},... | collective-permute-start | bytes 589832 | tf_op jit(solution)/shard_map/ppermute | solution.py:303
  13.7 13.8 %collective-permute-start = (bf16[768,128]{1,0:T(8,128)(2,1)S(1)}, bf16[768,128]{1,0:T(8,128)(2,1)S(1)}, u32[]{:S(2)}, u32[]{:S(2)}) collective-permute-start(bf16[768,128]{1,0:T(8,128)(2,1)S(1)} %copy-done.6), channel_id=1, source_target_pairs={{0,0},{1,4},{2,2},{3,6},{4,1},{5,5},{6,3},{7,7},{8,8},{9,12},{10,1... | collective-permute-start | bytes 589832 | tf_op jit(solution)/shard_map/ppermute | solution.py:303
  26.3 1.8 %collective-permute-start.6 = (bf16[768,128]{1,0:T(8,128)(2,1)S(1)}, bf16[768,128]{1,0:T(8,128)(2,1)S(1)}, u32[]{:S(2)}, u32[]{:S(2)}) collective-permute-start(bf16[768,128]{1,0:T(8,128)(2,1)S(1)} %collective-permute-done.5.rest_4_), channel_id=1, source_target_pairs={{0,1},{1,0},{2,3},{3,2},{4,5},{5,4},{6,7},{7,6},{8,9},{9,8},{10,11... | collective-permute-start | bytes 589832 | tf_op jit(solution)/shard_map/ppermute | solution.py:309
  27.0 1.4 %collective-permute-start.8 = (bf16[768,128]{1,0:T(8,128)(2,1)S(1)}, bf16[768,128]{1,0:T(8,128)(2,1)S(1)}, u32[]{:S(2)}, u32[]{:S(2)}) collective-permute-start(bf16[768,128]{1,0:T(8,128)(2,1)S(1)} %collective-permute-done.7.rest_6_), channel_id=1, source_target_pairs={{0,1},{1,0},{2,3},{3,2},{4,5},{5,4},{6,7},{7,6},{8,9},{9,8},{10,11... | collective-permute-start | bytes 589832 | tf_op jit(solution)/shard_map/ppermute | solution.py:309
  27.5 1.4 %collective-permute-start.4 = (bf16[768,128]{1,0:T(8,128)(2,1)S(1)}, bf16[768,128]{1,0:T(8,128)(2,1)S(1)}, u32[]{:S(2)}, u32[]{:S(2)}) collective-permute-start(bf16[768,128]{1,0:T(8,128)(2,1)S(1)} %collective-permute-done.3.rest_2_), channel_id=1, source_target_pairs={{0,1},{1,0},{2,3},{3,2},{4,5},{5,4},{6,7},{7,6},{8,9},{9,8},{10,11... | collective-permute-start | bytes 589832 | tf_op jit(solution)/shard_map/ppermute | solution.py:309
  27.6 1.6 %copy-start.4 = (s32[172]{0:T(256)S(1)}, s32[172]{0:T(256)}, u32[]{:S(2)}) copy-start(s32[172]{0:T(256)} %get-tuple-element.44.first) | copy-start | bytes 2068
  27.6 1.6 %copy-start = (s32[576]{0:T(1024)S(1)}, s32[576]{0:T(1024)}, u32[]{:S(2)}) copy-start(s32[576]{0:T(1024)} %get-tuple-element.42.which) | copy-start | bytes 6916
  27.6 1.6 %copy-start.2 = (s32[172]{0:T(256)S(1)}, s32[172]{0:T(256)}, u32[]{:S(2)}) copy-start(s32[172]{0:T(256)} %get-tuple-element.41.where) | copy-start | bytes 2068
  27.6 1.6 %copy-start.3 = (s32[172]{0:T(256)S(1)}, s32[172]{0:T(256)}, u32[]{:S(2)}) copy-start(s32[172]{0:T(256)} %get-tuple-element.43.valid) | copy-start | bytes 2068
  27.6 1.6 %copy-start.1 = (s32[172]{0:T(256)S(1)}, s32[172]{0:T(256)}, u32[]{:S(2)}) copy-start(s32[172]{0:T(256)} %get-tuple-element.40.who) | copy-start | bytes 2068
  27.6 1.6 %collective-permute-start.2 = (bf16[768,128]{1,0:T(8,128)(2,1)S(1)}, bf16[768,128]{1,0:T(8,128)(2,1)S(1)}, u32[]{:S(2)}, u32[]{:S(2)}) collective-permute-start(bf16[768,128]{1,0:T(8,128)(2,1)S(1)} %collective-permute-done.rest_0_), channel_id=1, source_target_pairs={{0,1},{1,0},{2,3},{3,2},{4,5},{5,4},{6,7},{7,6},{8,9},{9,8},{10,11... | collective-permute-start | bytes 589832 | tf_op jit(solution)/shard_map/ppermute | solution.py:309
  35.0 8.4 %collective-permute-start.9 = (bf16[256,128]{1,0:T(8,128)(2,1)S(1)}, bf16[256,128]{1,0:T(8,128)(2,1)S(1)}, u32[]{:S(2)}, u32[]{:S(2)}) collective-permute-start(bf16[256,128]{1,0:T(8,128)(2,1)S(1)} %get-tuple-element.47), channel_id=1, source_target_pairs={{0,0},{1,4},{2,2},{3,6},{4,1},{5,5},{6,3},{7,7},{8,8},{9,12},{10,1... | collective-permute-start | bytes 196616 | tf_op jit(solution)/shard_map/ppermute | solution.py:303
  35.7 8.6 %collective-permute-start.10 = (bf16[256,128]{1,0:T(8,128)(2,1)S(1)}, bf16[256,128]{1,0:T(8,128)(2,1)S(1)}, u32[]{:S(2)}, u32[]{:S(2)}) collective-permute-start(bf16[256,128]{1,0:T(8,128)(2,1)S(1)} %get-tuple-element.48), channel_id=1, source_target_pairs={{0,8},{1,12},{2,10},{3,14},{4,9},{5,13},{6,11},{7,15},{8,0},{9,4},... | collective-permute-start | bytes 196616 | tf_op jit(solution)/shard_map/ppermute | solution.py:303
  40.1 5.4 %collective-permute-start.11 = (bf16[256,128]{1,0:T(8,128)(2,1)S(1)}, bf16[256,128]{1,0:T(8,128)(2,1)S(1)}, u32[]{:S(2)}, u32[]{:S(2)}) collective-permute-start(bf16[256,128]{1,0:T(8,128)(2,1)S(1)} %get-tuple-element.49), channel_id=1, source_target_pairs={{0,16},{1,20},{2,18},{3,22},{4,17},{5,21},{6,19},{7,23},{8,24},{9,... | collective-permute-start | bytes 196616 | tf_op jit(solution)/shard_map/ppermute | solution.py:303
  42.1 6.8 %collective-permute-start.12 = (bf16[256,128]{1,0:T(8,128)(2,1)S(1)}, bf16[256,128]{1,0:T(8,128)(2,1)S(1)}, u32[]{:S(2)}, u32[]{:S(2)}) collective-permute-start(bf16[256,128]{1,0:T(8,128)(2,1)S(1)} %get-tuple-element.50), channel_id=1, source_target_pairs={{0,24},{1,28},{2,26},{3,30},{4,25},{5,29},{6,27},{7,31},{8,16},{9,... | collective-permute-start | bytes 196616 | tf_op jit(solution)/shard_map/ppermute | solution.py:303
  43.5 6.1 %collective-permute-start.13 = (bf16[256,128]{1,0:T(8,128)(2,1)S(1)}, bf16[256,128]{1,0:T(8,128)(2,1)S(1)}, u32[]{:S(2)}, u32[]{:S(2)}) collective-permute-start(bf16[256,128]{1,0:T(8,128)(2,1)S(1)} %collective-permute-done.9.refs_0_), channel_id=1, source_target_pairs={{0,2},{1,3},{2,0},{3,1},{4,6},{5,7},{6,4},{7,5},{8,10},{9,11},{10,... | collective-permute-start | bytes 196616 | tf_op jit(solution)/shard_map/ppermute | solution.py:312
  44.3 5.3 %collective-permute-start.14 = (bf16[256,128]{1,0:T(8,128)(2,1)S(1)}, bf16[256,128]{1,0:T(8,128)(2,1)S(1)}, u32[]{:S(2)}, u32[]{:S(2)}) collective-permute-start(bf16[256,128]{1,0:T(8,128)(2,1)S(1)} %collective-permute-done.10.refs_1_), channel_id=1, source_target_pairs={{0,2},{1,3},{2,0},{3,1},{4,6},{5,7},{6,4},{7,5},{8,10},{9,11},{10,... | collective-permute-start | bytes 196616 | tf_op jit(solution)/shard_map/ppermute | solution.py:312
  45.5 4.5 %collective-permute-start.15 = (bf16[256,128]{1,0:T(8,128)(2,1)S(1)}, bf16[256,128]{1,0:T(8,128)(2,1)S(1)}, u32[]{:S(2)}, u32[]{:S(2)}) collective-permute-start(bf16[256,128]{1,0:T(8,128)(2,1)S(1)} %collective-permute-done.11.refs_2_), channel_id=1, source_target_pairs={{0,2},{1,3},{2,0},{3,1},{4,6},{5,7},{6,4},{7,5},{8,10},{9,11},{10,... | collective-permute-start | bytes 196616 | tf_op jit(solution)/shard_map/ppermute | solution.py:312
  48.9 4.3 %collective-permute-start.16 = (bf16[256,128]{1,0:T(8,128)(2,1)S(1)}, bf16[256,128]{1,0:T(8,128)(2,1)S(1)}, u32[]{:S(2)}, u32[]{:S(2)}) collective-permute-start(bf16[256,128]{1,0:T(8,128)(2,1)S(1)} %collective-permute-done.12.refs_3_), channel_id=1, source_target_pairs={{0,2},{1,3},{2,0},{3,1},{4,6},{5,7},{6,4},{7,5},{8,10},{9,11},{10,... | collective-permute-start | bytes 196616 | tf_op jit(solution)/shard_map/ppermute | solution.py:312
  53.5 2.0 %collective-permute-start.17 = (bf16[512,256]{1,0:T(8,128)(2,1)S(1)}, bf16[512,256]{1,0:T(8,128)(2,1)S(1)}, u32[]{:S(2)}, u32[]{:S(2)}) collective-permute-start(bf16[512,256]{1,0:T(8,128)(2,1)S(1)} %shard_map.75), channel_id=1, source_target_pairs={{0,1},{1,0},{2,3},{3,2},{4,5},{5,4},{6,7},{7,6},{8,9},{9,8},{10,11... | collective-permute-start | bytes 786440 | tf_op jit(solution)/shard_map/ppermute | solution.py:312
where the time goes:
time: 57.4 us; the launch traced here: 56.6 us
  starting transfers between devices  22.2 us (39%)
  Pallas kernels  17.2 us (30%)
  waiting for transfers between devices  16.9 us (29%)
    ppermute x8, starting transfers between devices, turn(): return lax.ppermute(x, both, pairs)  13.4 us
    ppermute x8, waiting for transfers between devices, turn(): return lax.ppermute(x, both, pairs)  11.1 us
    ppermute x6, starting transfers between devices, head_swap(): lax.ppermute(x, 'head', [(h, h ^ j) for h in range(groups)])  7.44 us
    pallas_call x2, Pallas kernels, body(): pl.pallas_call(functools.partial(proj_kernel, inner, far), out_shape=[jax...  6.27 us
    pallas_call x1, Pallas kernels, body(): pl.pallas_call(functools.partial(attend_kernel, per, cap, len(kv), rows,...  5.8 us
    ppermute x6, waiting for transfers between devices, head_swap(): lax.ppermute(x, 'head', [(h, h ^ j) for h in range(groups)])  4.69 us
    pallas_call x1, Pallas kernels, body(): pl.pallas_call(functools.partial(list_kernel, inner, heads, per, cap), ou...  3.72 us
    pallas_call x2, Pallas kernels, out(): pl.pallas_call(functools.partial(out_kernel, inner, heads, groups // 2, o...  1.44 us
  transfers between devices with their start and end apart: 18, of which 9 were waited for; matrix products, arithmetic and copies ran while one was open for 0% of the time, Pallas kernels for 7%

commit v1 on v0

--- a/solution.py
+++ b/solution.py
@@ -13,6 +13,7 @@
 LANES = 128
 SLOTS = 4
 STREAMS = 4
+TALL = HEAD_DIM + 16
 NEG = -1e30
 
 
@@ -155,10 +156,11 @@
     ins, rest = rest[:n_kv], rest[n_kv:]
     q_in = ins[:: n_kv // n_q]
     outs, rest = rest[:n_q], rest[n_q:]
-    kq, vt, qt, sc, m_s, al_s, l_s, acc_s, l_all, acc_all = rest
+    kq, vt, qt, sc, m_s, al_s, acc_s, acc_all = rest
     half = per // 2
     nq = n_q * per
     zero = jnp.zeros((HEAD_DIM, BLOCK), jnp.bfloat16)
+    ones = jnp.ones((TALL - HEAD_DIM, BLOCK), jnp.bfloat16)
     for k, msg in enumerate(q_in):
         for i in range(per):
             turned = msg[start_q + i * HEAD_DIM : start_q + (i + 1) * HEAD_DIM, :]
@@ -170,91 +172,82 @@
             kq[n * half + r] = msg[r * BLOCK : (r + 1) * BLOCK, :]
         for i in range(per):
             start = half * BLOCK + (i // 2 + i % 2 * half) * HEAD_DIM
-            vt[n * per + i] = msg[start : start + HEAD_DIM, :]
+            vt[n * per + i, :HEAD_DIM] = msg[start : start + HEAD_DIM, :]
+            vt[n * per + i, HEAD_DIM:] = ones
     m_s[...] = jnp.full(m_s.shape, NEG, jnp.float32)
-    l_s[...] = jnp.zeros(l_s.shape, jnp.float32)
     acc_s[...] = jnp.zeros(acc_s.shape, jnp.float32)
 
     def keys(s, t):
         start = where[s * cap + t]
         return [which[start + e] for e in range(SLOTS)]
 
-    def score(t, buf):
-        for s in range(STREAMS):
-            qi = who[s * cap + t]
-            tiles = []
-            for e, slot in enumerate(keys(s, t)):
-                tile = jnp.dot(
-                    kq[slot >> 1], qt[slot & 1, qi], preferred_element_type=jnp.float32
-                )
-                sc[buf, s, e] = tile
-                tiles.append(tile.reshape(BLOCK // 8, 8, BLOCK))
-            top = jnp.max(functools.reduce(jnp.maximum, tiles), axis=0)
-            top = jnp.max(top, axis=0, keepdims=True)
-            m_old = jnp.where(first[s * cap + t] == 1, NEG, m_s[1 - buf, s])
-            m_new = jnp.maximum(m_old, top)
-            al_s[buf, s] = jnp.exp(m_old - m_new)
-            m_s[buf, s] = m_new
-
-    def weigh(t, buf):
-        for s in range(STREAMS):
-            qi = who[s * cap + t]
-            n_valid = valid[s * cap + t]
-            m, alpha = m_s[buf, s], al_s[buf, s]
-            acc = acc_s[s] * alpha
-            total = l_s[s] * alpha
-            ids = keys(s, t)
-            for e in range(0, SLOTS, 2):
-                probs = []
-                for f in (e, e + 1):
-                    shut = m + jnp.where(f < n_valid, 0.0, -NEG)
-                    p = jnp.exp(sc[buf, s, f] - shut)
-                    total = total + jnp.sum(p.reshape(BLOCK // 8, 8, BLOCK), axis=0)
-                    probs.append(p.astype(jnp.bfloat16))
-                acc = acc + jnp.dot(
-                    jnp.concatenate([vt[ids[e]], vt[ids[e + 1]]], axis=1),
-                    jnp.concatenate(probs, axis=0),
-                    preferred_element_type=jnp.float32,
-                )
-            acc_s[s] = acc
-            l_s[s] = total
-            acc_all[qi] = acc
-            l_all[qi] = total
-
-    score(0, 0)
+    def score(t, buf, s):
+        qi = who[s * cap + t]
+        tiles = []
+        for e, slot in enumerate(keys(s, t)):
+            tile = jnp.dot(kq[slot >> 1], qt[slot & 1, qi], preferred_element_type=jnp.float32)
+            sc[buf, s, e] = tile
+            tiles.append(tile.reshape(BLOCK // 8, 8, BLOCK))
+        top = jnp.max(functools.reduce(jnp.maximum, tiles), axis=0)
+        top = jnp.max(top, axis=0, keepdims=True)
+        m_old = jnp.where(first[s * cap + t] == 1, NEG, m_s[1 - buf, s])
+        m_new = jnp.maximum(m_old, top)
+        al_s[buf, s] = jnp.exp(m_old - m_new)
+        m_s[buf, s] = m_new
+
+    def weigh(t, buf, s):
+        qi = who[s * cap + t]
+        n_valid = valid[s * cap + t]
+        m, alpha = m_s[buf, s], al_s[buf, s]
+        acc = acc_s[s] * alpha
+        ids = keys(s, t)
+        for e in range(0, SLOTS, 2):
+            probs = []
+            for f in (e, e + 1):
+                shut = m + jnp.where(f < n_valid, 0.0, -NEG)
+                probs.append(jnp.exp(sc[buf, s, f] - shut).astype(jnp.bfloat16))
+            acc = acc + jnp.dot(
+                jnp.concatenate([vt[ids[e]], vt[ids[e + 1]]], axis=1),
+                jnp.concatenate(probs, axis=0),
+                preferred_element_type=jnp.float32,
+            )
+        acc_s[s] = acc
+        acc_all[qi] = acc
+
+    for s in range(STREAMS):
+        score(0, 0, s)
     count = steps[0]
 
     def step(u, _):
-        t = 2 * u
-        score(t + 1, 1)
-        weigh(t, 0)
-        score(t + 2, 0)
-        weigh(t + 1, 1)
+        for buf in (0, 1):
+            for s in range(STREAMS):
+                score(2 * u + 1 + buf, 1 - buf, s)
+                weigh(2 * u + buf, buf, s)
         return 0
 
     lax.fori_loop(0, lax.div(count, 2), step, 0)
 
     @pl.when(lax.rem(count, 2) == 1)
     def _():
-        weigh(count - 1, 0)
+        for s in range(STREAMS):
+            weigh(count - 1, 0, s)
 
     for k in range(n_q):
         for r in range(half):
             done = []
             for i in (k * per + r, k * per + r + half):
-                done.append(acc_all[i] * (1.0 / jnp.sum(l_all[i], axis=0, keepdims=True)))
+                total = acc_all[i]
+                done.append(total[:HEAD_DIM] * (1.0 / total[HEAD_DIM : HEAD_DIM + 1]))
             outs[k][r * BLOCK : (r + 1) * BLOCK, :] = jnp.transpose(
                 jnp.concatenate(done, axis=0)
             ).astype(jnp.bfloat16)
 
 
-def out_kernel(inner, heads, groups, other, *refs):
+def out_kernel(inner, heads, groups, *refs):
     pieces = [refs[g * heads : (g + 1) * heads] for g in range(groups)]
     ws = refs[groups * heads : groups * heads + groups]
     out = refs[-1]
     a = lax.axis_index("ctx") // inner
-    side = (lax.axis_index("head") % 2) ^ other
-    cols = pl.ds(pl.multiple_of(side * out.shape[1], LANES), out.shape[1])
     half = pieces[0][0].shape[0]
     low = low_half((half, LANES))
     tops, bottoms, rows = [], [], []
@@ -266,14 +259,13 @@
             bottoms.append(jnp.where(low, swap_halves(p0), p1).astype(jnp.bfloat16))
             for e in (0, 1):
                 start = pl.multiple_of(HEAD_DIM * (a ^ (k + e)), HEAD_DIM)
-                rows.append(ws[g][pl.ds(start, HEAD_DIM), cols])
+                rows.append(ws[g][pl.ds(start, HEAD_DIM), :])
     w = jnp.concatenate(rows, axis=0)
     for n, parts in enumerate((tops, bottoms)):
         x = jnp.concatenate(parts, axis=1)
-        total = jnp.dot(x, w, preferred_element_type=jnp.float32)
-        if not other:
-            total = total + refs[-2][n * half : (n + 1) * half, :].astype(jnp.float32)
-        out[n * half : (n + 1) * half, :] = total.astype(out.dtype)
+        out[n * half : (n + 1) * half, :] = jnp.dot(
+            x, w, preferred_element_type=jnp.float32
+        ).astype(out.dtype)
 
 
 def solution(mesh):
@@ -352,13 +344,13 @@
             ],
             name="block_lists",
         )(block_mask, block_order)
-        x = lax.axis_index("head") // 2
+        h = lax.axis_index("head")
         w_out, msgs = lax.optimization_barrier((w_out, msgs))
         w_cols = []
-        for g in range(0, groups, 2):
-            share = lax.dynamic_slice_in_dim(w_out, (x ^ g // 2) * 2 * cols, 2 * cols, axis=1)
+        for g in range(groups):
+            share = lax.dynamic_slice_in_dim(w_out, (h ^ g) * cols, cols, axis=1)
             w_cols.append(head_swap(share, g))
-        got[0], tables, w_cols = lax.optimization_barrier((got[0], tables, w_cols))
+        got[0], tables = lax.optimization_barrier((got[0], tables))
         kv = []
         for j in range(heads):
             for e in range(inner):
@@ -370,15 +362,13 @@
             out_specs=[VMEM] * heads,
             scratch_shapes=[
                 pltpu.VMEM((nb // 2, BLOCK, LANES), bf),
-                pltpu.VMEM((nb, HEAD_DIM, BLOCK), bf),
+                pltpu.VMEM((nb, TALL, BLOCK), bf),
                 pltpu.VMEM((2, nq + 1, LANES, BLOCK), bf),
                 pltpu.VMEM((2, STREAMS, SLOTS, BLOCK, BLOCK), jnp.float32),
                 pltpu.VMEM((2, STREAMS, 1, BLOCK), jnp.float32),
                 pltpu.VMEM((2, STREAMS, 1, BLOCK), jnp.float32),
-                pltpu.VMEM((STREAMS, 8, BLOCK), jnp.float32),
-                pltpu.VMEM((STREAMS, HEAD_DIM, BLOCK), jnp.float32),
-                pltpu.VMEM((nq + 1, 8, BLOCK), jnp.float32),
-                pltpu.VMEM((nq + 1, HEAD_DIM, BLOCK), jnp.float32),
+                pltpu.VMEM((STREAMS, TALL, BLOCK), jnp.float32),
+                pltpu.VMEM((nq + 1, TALL, BLOCK), jnp.float32),
             ],
             compiler_params=params,
             name="attend",
@@ -386,21 +376,20 @@
         mine = [None] * heads
         for j in reversed(range(heads)):
             mine[j] = turn(o[j], j)
-        pieces = []
-        for g in range(0, groups, 2):
+        parts = [mine]
+        for g in range(1, groups):
+            part = []
             for j in range(heads):
-                pieces.append(head_swap(mine[j], g))
-
-        def out(other, *more):
-            return pl.pallas_call(
-                functools.partial(out_kernel, inner, heads, groups // 2, other),
-                out_shape=jax.ShapeDtypeStruct((rows, cols), bf),
-                in_specs=[VMEM] * (len(pieces) + len(w_cols) + len(more)),
-                out_specs=VMEM,
-                compiler_params=params,
-            )(*pieces, *w_cols, *more)
-
-        return out(0, head_swap(out(1), 1))
+                part.append(head_swap(parts[g - 1][j], 1) if g % 2 else head_swap(mine[j], g))
+            parts.append(part)
+        return pl.pallas_call(
+            functools.partial(out_kernel, inner, heads, groups),
+            out_shape=jax.ShapeDtypeStruct((rows, cols), bf),
+            in_specs=[VMEM] * (groups * heads + groups),
+            out_specs=VMEM,
+            compiler_params=params,
+            name="out_proj",
+        )(*[x for part in parts for x in part], *w_cols)
 
     placed = (
         P("ctx", None),

time: 57.4 us -> 59.2 us (1.031)
  starting transfers between devices: 22.2 us -> 30.6 us
  waiting for transfers between devices: 16.9 us -> 11.2 us
    ppermute x6 -> x15, starting transfers between devices: 7.44 us -> 12.6 us  [head_swap(): lax.ppermute(x, 'head', [(h, h ^ j) for h in range(groups)])]
    ppermute x8, waiting for transfers between devices: 11.1 us -> 7.54 us  [turn(): return lax.ppermute(x, both, pairs)]
    ppermute x8, starting transfers between devices: 13.4 us -> 15.9 us  [turn(): return lax.ppermute(x, both, pairs)]
    ppermute x4, waiting for transfers between devices: 1.09 us -> 0.01 us  [spread(): return lax.ppermute(x, both, pairs) if e else x]
    ppermute x6 -> x15, waiting for transfers between devices: 4.69 us -> 3.63 us  [head_swap(): lax.ppermute(x, 'head', [(h, h ^ j) for h in range(groups)])]
    ppermute x4, starting transfers between devices: 1.35 us -> 2.04 us  [spread(): return lax.ppermute(x, both, pairs) if e else x]
    pallas_call x2 -> x1, Pallas kernels: 1.44 us -> 1.27 us  [body(): pl.pallas_call(functools.partial(out_kernel, inner, heads, groups), out_s...]
  transfers between devices with their start and end apart: 18 -> 27, of which waited for: 9 -> 4; matrix products, arithmetic and copies ran while one was open for 0% -> 0% of each run, Pallas kernels for 7% -> 21%
where the time goes in v1:
time: 59.2 us; the launch traced here: 58.9 us
  starting transfers between devices  30.6 us (52%)
  Pallas kernels  16.8 us (28%)
  waiting for transfers between devices  11.2 us (19%)
    ppermute x8, starting transfers between devices, turn(): return lax.ppermute(x, both, pairs)  15.9 us
    ppermute x15, starting transfers between devices, head_swap(): lax.ppermute(x, 'head', [(h, h ^ j) for h in range(groups)])  12.6 us
    ppermute x8, waiting for transfers between devices, turn(): return lax.ppermute(x, both, pairs)  7.54 us
    pallas_call x2, Pallas kernels, body(): pl.pallas_call(functools.partial(proj_kernel, inner, far), out_shape=[jax...  6.21 us
    pallas_call x1, Pallas kernels, body(): pl.pallas_call(functools.partial(attend_kernel, per, cap, len(kv), rows,...  5.65 us
    pallas_call x1, Pallas kernels, body(): pl.pallas_call(functools.partial(list_kernel, inner, heads, per, cap), ou...  3.71 us
    ppermute x15, waiting for transfers between devices, head_swap(): lax.ppermute(x, 'head', [(h, h ^ j) for h in range(groups)])  3.63 us
    ppermute x4, starting transfers between devices, spread(): return lax.ppermute(x, both, pairs) if e else x  2.04 us
  transfers between devices with their start and end apart: 27, of which 4 were waited for; matrix products, arithmetic and copies ran while one was open for 0% of the time, Pallas kernels for 21%

profile of v1, /device:TPU:0, one launch (start us, length us, event | category | flops | bytes accessed | tf_op | source)
XLA Modules:
  0.0 58.9 jit_solution(9416174960038967087)
XLA Ops:
  0.0 3.1 %shard_map.74 = (bf16[768,128]{1,0:T(8,128)(2,1)}, bf16[768,128]{1,0:T(8,128)(2,1)}) custom-call(bf16[512,1024]{1,0:T(8,128)(2,1)} %tok_in.3, bf16[1024,256]{1,0:T(8,128)(2,1)} %wk_in.3, bf16[1024,256]{1,0:T(8,128)(2,1)} %wv_in.3, bf16[1024,256]{1,0:T(8,128)(2,1)} %wq_in.3), custom_call_target="tpu_custom_call" | custom-call | tf_op jit(solution)/shard_map/pallas_call | solution.py:309
  3.1 4.1 %collective-permute-start.4 = (bf16[768,128]{1,0:T(8,128)(2,1)}, bf16[768,128]{1,0:T(8,128)(2,1)S(1)}, u32[]{:S(2)}, u32[]{:S(2)}) collective-permute-start(bf16[768,128]{1,0:T(8,128)(2,1)} %get-tuple-element.42), channel_id=1, source_target_pairs={{0,16},{1,20},{2,18},{3,22},{4,17},{5,21},{6,19},{7,23},{8,24},{9,... | collective-permute-start | bytes 589832 | tf_op jit(solution)/shard_map/ppermute | solution.py:295
  7.3 1.3 %collective-permute-start.6 = (bf16[768,128]{1,0:T(8,128)(2,1)}, bf16[768,128]{1,0:T(8,128)(2,1)S(1)}, u32[]{:S(2)}, u32[]{:S(2)}) collective-permute-start(bf16[768,128]{1,0:T(8,128)(2,1)} %get-tuple-element.43), channel_id=1, source_target_pairs={{0,24},{1,28},{2,26},{3,30},{4,25},{5,29},{6,27},{7,31},{8,16},{9,... | collective-permute-start | bytes 589832 | tf_op jit(solution)/shard_map/ppermute | solution.py:295
  8.6 3.1 %shard_map.73 = (bf16[768,128]{1,0:T(8,128)(2,1)}, bf16[768,128]{1,0:T(8,128)(2,1)}) custom-call(bf16[512,1024]{1,0:T(8,128)(2,1)} %tok_in.3, bf16[1024,256]{1,0:T(8,128)(2,1)} %wk_in.3, bf16[1024,256]{1,0:T(8,128)(2,1)} %wv_in.3, bf16[1024,256]{1,0:T(8,128)(2,1)} %wq_in.3), custom_call_target="tpu_custom_call" | custom-call | tf_op jit(solution)/shard_map/pallas_call | solution.py:309
  11.7 1.6 %collective-permute-start = (bf16[768,128]{1,0:T(8,128)(2,1)}, bf16[768,128]{1,0:T(8,128)(2,1)S(1)}, u32[]{:S(2)}, u32[]{:S(2)}) collective-permute-start(bf16[768,128]{1,0:T(8,128)(2,1)} %get-tuple-element.27), channel_id=1, source_target_pairs={{0,0},{1,4},{2,2},{3,6},{4,1},{5,5},{6,3},{7,7},{8,8},{9,12},{10,1... | collective-permute-start | bytes 589832 | tf_op jit(solution)/shard_map/ppermute | solution.py:295
  13.3 0.3 collective-permute-start.2
  13.6 7.4 %collective-permute-done.4.rest_4_ = bf16[768,128]{1,0:T(8,128)(2,1)S(1)} collective-permute-done((bf16[768,128]{1,0:T(8,128)(2,1)}, bf16[768,128]{1,0:T(8,128)(2,1)S(1)}, u32[]{:S(2)}, u32[]{:S(2)}) %collective-permute-start.4) | collective-permute-done | bytes 196640 | tf_op jit(solution)/shard_map/ppermute | solution.py:295
  21.0 1.4 %collective-permute-start.5 = (bf16[768,128]{1,0:T(8,128)(2,1)S(1)}, bf16[768,128]{1,0:T(8,128)(2,1)S(1)}, u32[]{:S(2)}, u32[]{:S(2)}) collective-permute-start(bf16[768,128]{1,0:T(8,128)(2,1)S(1)} %collective-permute-done.4.rest_4_), channel_id=1, source_target_pairs={{0,1},{1,0},{2,3},{3,2},{4,5},{5,4},{6,7},{7,6},{8,9},{9,8},{10,11... | collective-permute-start | bytes 589832 | tf_op jit(solution)/shard_map/ppermute | solution.py:301
  22.5 0.0 collective-permute-done.6.rest_6_
  22.5 0.0 collective-permute-start.7
  22.5 3.7 %block_lists.1 = (s32[172]{0:T(256)}, s32[172]{0:T(256)}, s32[576]{0:T(1024)}, s32[172]{0:T(256)}, s32[172]{0:T(256)}, /*index=5*/s32[1]{0:T(128)}) custom-call(s32[32,32]{1,0:T(8,128)} %mask.1, s32[32]{0:T(128)} %order.1), custom_call_target="tpu_custom_call" | custom-call | tf_op jit(solution)/shard_map/block_lists/pallas_call | solution.py:328
  26.2 0.0 collective-permute-done.rest_0_
  26.2 0.5 collective-permute-start.1
  26.7 0.0 collective-permute-done.2.rest_2_
  26.7 0.1 collective-permute-start.3
  26.8 0.0 copy-done.5
  26.8 0.1 constant_dynamic-slice_fusion
  26.9 0.0 copy-start
  26.9 1.6 %collective-permute-start.26 = (bf16[256,256]{1,0:T(8,128)(2,1)S(1)}, bf16[256,256]{1,0:T(8,128)(2,1)S(1)}, u32[]{:S(2)}, u32[]{:S(2)}) collective-permute-start(bf16[256,256]{1,0:T(8,128)(2,1)S(1)} %get-tuple-element.49), channel_id=1, source_target_pairs={{0,3},{1,2},{2,1},{3,0},{4,7},{5,6},{6,5},{7,4},{8,11},{9,10},{10,... | collective-permute-start | bytes 393224 | tf_op jit(solution)/shard_map/ppermute | solution.py:304
  28.5 0.0 collective-permute-done.5.rest_5_
  28.5 0.5 collective-permute-start.25
  29.1 0.0 collective-permute-done.7.rest_7_
  29.1 0.0 collective-permute-start.24
  29.1 0.0 collective-permute-done.1.rest_1_
  29.1 0.0 collective-permute-done.3.rest_3_
  29.1 0.0 copy-done.2
  29.1 0.1 copy-done.1
  29.2 5.7 %attend.1 = (bf16[256,128]{1,0:T(8,128)(2,1)S(1)}, bf16[256,128]{1,0:T(8,128)(2,1)S(1)}, bf16[256,128]{1,0:T(8,128)(2,1)S(1)}, bf16[256,128]{1,0:T(8,128)(2,1)S(1)}) custom-call(s32[172]{0:T(256)S(1)} %copy-done.1, s32[172]{0:T(256)S(1)} %copy-done.2, s32[576]{0:T(1024)S(1)} %copy-done, s32[172]{0:T(256)S(1)} %copy-done.3, s32[172]{0:T(256)S(1)} %copy-done.4, ...), custom_call_target="tpu_custom_call" | custom-call | tf_op jit(solution)/shard_map/attend/pallas_call | solution.py:358
  34.9 0.7 %collective-permute-start.8 = (bf16[256,128]{1,0:T(8,128)(2,1)S(1)}, bf16[256,128]{1,0:T(8,128)(2,1)S(1)}, u32[]{:S(2)}, u32[]{:S(2)}) collective-permute-start(bf16[256,128]{1,0:T(8,128)(2,1)S(1)} %get-tuple-element.44), channel_id=1, source_target_pairs={{0,0},{1,4},{2,2},{3,6},{4,1},{5,5},{6,3},{7,7},{8,8},{9,12},{10,1... | collective-permute-start | bytes 196616 | tf_op jit(solution)/shard_map/ppermute | solution.py:295
  35.5 4.6 %collective-permute-start.9 = (bf16[256,128]{1,0:T(8,128)(2,1)S(1)}, bf16[256,128]{1,0:T(8,128)(2,1)S(1)}, u32[]{:S(2)}, u32[]{:S(2)}) collective-permute-start(bf16[256,128]{1,0:T(8,128)(2,1)S(1)} %get-tuple-element.45), channel_id=1, source_target_pairs={{0,8},{1,12},{2,10},{3,14},{4,9},{5,13},{6,11},{7,15},{8,0},{9,4},... | collective-permute-start | bytes 196616 | tf_op jit(solution)/shard_map/ppermute | solution.py:295
  40.1 0.0 collective-permute-done.26.refs_19_
  40.1 1.9 %collective-permute-start.10 = (bf16[256,128]{1,0:T(8,128)(2,1)S(1)}, bf16[256,128]{1,0:T(8,128)(2,1)S(1)}, u32[]{:S(2)}, u32[]{:S(2)}) collective-permute-start(bf16[256,128]{1,0:T(8,128)(2,1)S(1)} %get-tuple-element.46), channel_id=1, source_target_pairs={{0,16},{1,20},{2,18},{3,22},{4,17},{5,21},{6,19},{7,23},{8,24},{9,... | collective-permute-start | bytes 196616 | tf_op jit(solution)/shard_map/ppermute | solution.py:295
  42.0 0.0 collective-permute-done.25.refs_18_
  42.0 1.4 %collective-permute-start.11 = (bf16[256,128]{1,0:T(8,128)(2,1)S(1)}, bf16[256,128]{1,0:T(8,128)(2,1)S(1)}, u32[]{:S(2)}, u32[]{:S(2)}) collective-permute-start(bf16[256,128]{1,0:T(8,128)(2,1)S(1)} %get-tuple-element.47), channel_id=1, source_target_pairs={{0,24},{1,28},{2,26},{3,30},{4,25},{5,29},{6,27},{7,31},{8,16},{9,... | collective-permute-start | bytes 196616 | tf_op jit(solution)/shard_map/ppermute | solution.py:295
  43.4 0.0 collective-permute-done.8.refs_0_
  43.4 1.5 %collective-permute-start.16 = (bf16[256,128]{1,0:T(8,128)(2,1)S(1)}, bf16[256,128]{1,0:T(8,128)(2,1)S(1)}, u32[]{:S(2)}, u32[]{:S(2)}) collective-permute-start(bf16[256,128]{1,0:T(8,128)(2,1)S(1)} %collective-permute-done.8.refs_0_), channel_id=1, source_target_pairs={{0,2},{1,3},{2,0},{3,1},{4,6},{5,7},{6,4},{7,5},{8,10},{9,11},{10,... | collective-permute-start | bytes 196616 | tf_op jit(solution)/shard_map/ppermute | solution.py:304
  44.9 0.0 collective-permute-done.24.refs_17_
  44.9 3.2 %collective-permute-start.12 = (bf16[256,128]{1,0:T(8,128)(2,1)S(1)}, bf16[256,128]{1,0:T(8,128)(2,1)S(1)}, u32[]{:S(2)}, u32[]{:S(2)}) collective-permute-start(bf16[256,128]{1,0:T(8,128)(2,1)S(1)} %collective-permute-done.8.refs_0_), channel_id=1, source_target_pairs={{0,1},{1,0},{2,3},{3,2},{4,5},{5,4},{6,7},{7,6},{8,9},{9,8},{10,11... | collective-permute-start | bytes 196616 | tf_op jit(solution)/shard_map/ppermute | solution.py:304
  48.1 0.0 collective-permute-done.9.refs_1_
  48.1 0.6 %collective-permute-start.17 = (bf16[256,128]{1,0:T(8,128)(2,1)S(1)}, bf16[256,128]{1,0:T(8,128)(2,1)S(1)}, u32[]{:S(2)}, u32[]{:S(2)}) collective-permute-start(bf16[256,128]{1,0:T(8,128)(2,1)S(1)} %collective-permute-done.9.refs_1_), channel_id=1, source_target_pairs={{0,2},{1,3},{2,0},{3,1},{4,6},{5,7},{6,4},{7,5},{8,10},{9,11},{10,... | collective-permute-start | bytes 196616 | tf_op jit(solution)/shard_map/ppermute | solution.py:304
  48.7 0.0 collective-permute-done.10.refs_2_
  48.7 0.1 collective-permute-start.13
  48.8 0.1 collective-permute-done.11.refs_3_
  48.9 1.5 %collective-permute-start.18 = (bf16[256,128]{1,0:T(8,128)(2,1)S(1)}, bf16[256,128]{1,0:T(8,128)(2,1)S(1)}, u32[]{:S(2)}, u32[]{:S(2)}) collective-permute-start(bf16[256,128]{1,0:T(8,128)(2,1)S(1)} %collective-permute-done.10.refs_2_), channel_id=1, source_target_pairs={{0,2},{1,3},{2,0},{3,1},{4,6},{5,7},{6,4},{7,5},{8,10},{9,11},{10,... | collective-permute-start | bytes 196616 | tf_op jit(solution)/shard_map/ppermute | solution.py:304
  50.3 0.0 collective-permute-done.16.refs_8_
  50.3 1.8 %collective-permute-start.14 = (bf16[256,128]{1,0:T(8,128)(2,1)S(1)}, bf16[256,128]{1,0:T(8,128)(2,1)S(1)}, u32[]{:S(2)}, u32[]{:S(2)}) collective-permute-start(bf16[256,128]{1,0:T(8,128)(2,1)S(1)} %collective-permute-done.10.refs_2_), channel_id=1, source_target_pairs={{0,1},{1,0},{2,3},{3,2},{4,5},{5,4},{6,7},{7,6},{8,9},{9,8},{10,11... | collective-permute-start | bytes 196616 | tf_op jit(solution)/shard_map/ppermute | solution.py:304
  52.1 0.0 collective-permute-done.12.refs_4_
  52.1 0.5 collective-permute-start.19
  52.7 0.0 collective-permute-done.17.refs_9_
  52.7 0.0 collective-permute-start.15
  52.7 0.0 collective-permute-done.13.refs_5_
  52.7 0.5 collective-permute-start.20
  53.2 0.0 collective-permute-done.18.refs_10_
  53.2 0.8 %collective-permute-start.21 = (bf16[256,128]{1,0:T(8,128)(2,1)S(1)}, bf16[256,128]{1,0:T(8,128)(2,1)S(1)}, u32[]{:S(2)}, u32[]{:S(2)}) collective-permute-start(bf16[256,128]{1,0:T(8,128)(2,1)S(1)} %collective-permute-done.17.refs_9_), channel_id=1, source_target_pairs={{0,1},{1,0},{2,3},{3,2},{4,5},{5,4},{6,7},{7,6},{8,9},{9,8},{10,11... | collective-permute-start | bytes 196616 | tf_op jit(solution)/shard_map/ppermute | solution.py:304
  54.0 0.0 collective-permute-done.14.refs_6_
  54.0 0.0 collective-permute-start.22
  54.0 2.4 %collective-permute-done.19.refs_11_ = bf16[256,128]{1,0:T(8,128)(2,1)S(1)} collective-permute-done((bf16[256,128]{1,0:T(8,128)(2,1)S(1)}, bf16[256,128]{1,0:T(8,128)(2,1)S(1)}, u32[]{:S(2)}, u32[]{:S(2)}) %collective-permute-start.19) | collective-permute-done | bytes 65568 | tf_op jit(solution)/shard_map/ppermute | solution.py:304
  56.4 0.0 collective-permute-start.23
  56.4 0.0 collective-permute-done.15.refs_7_
  56.4 0.0 collective-permute-done.20.refs_12_
  56.4 0.0 collective-permute-done.21.refs_13_
  56.4 0.0 collective-permute-done.22.refs_14_
  56.4 1.2 %collective-permute-done.23.refs_15_ = bf16[256,128]{1,0:T(8,128)(2,1)S(1)} collective-permute-done((bf16[256,128]{1,0:T(8,128)(2,1)S(1)}, bf16[256,128]{1,0:T(8,128)(2,1)S(1)}, u32[]{:S(2)}, u32[]{:S(2)}) %collective-permute-start.23) | collective-permute-done | bytes 65568 | tf_op jit(solution)/shard_map/ppermute | solution.py:304
  57.7 1.3 %out_proj.1 = bf16[512,256]{1,0:T(8,128)(2,1)} custom-call(bf16[256,128]{1,0:T(8,128)(2,1)S(1)} %collective-permute-done.8.refs_0_, bf16[256,128]{1,0:T(8,128)(2,1)S(1)} %collective-permute-done.9.refs_1_, bf16[256,128]{1,0:T(8,128)(2,1)S(1)} %collective-permute-done.10.refs_2_, bf16[256,128]{1,0:T(8,128)(2,1)S(1)} %collective-permute-done.11.refs_3_, ...), custom_call_target="tpu_custom_call" | custom-call | tf_op jit(solution)/shard_map/out_proj/pallas_call | solution.py:385
  (8 shorter events, 0.0 us)
Async XLA Ops:
  3.1 17.9 %collective-permute-start.4 = (bf16[768,128]{1,0:T(8,128)(2,1)}, bf16[768,128]{1,0:T(8,128)(2,1)S(1)}, u32[]{:S(2)}, u32[]{:S(2)}) collective-permute-start(bf16[768,128]{1,0:T(8,128)(2,1)} %get-tuple-element.42), channel_id=1, source_target_pairs={{0,16},{1,20},{2,18},{3,22},{4,17},{5,21},{6,19},{7,23},{8,24},{9,... | collective-permute-start | bytes 589832 | tf_op jit(solution)/shard_map/ppermute | solution.py:295
  7.3 19.6 %copy-start.5 = (bf16[256,1024]{1,0:T(8,128)(2,1)S(1)}, bf16[256,1024]{1,0:T(8,128)(2,1)}, u32[]{:S(2)}) copy-start(bf16[256,1024]{1,0:T(8,128)(2,1)} %param.11) | copy-start | bytes 1572868
  7.3 15.2 %collective-permute-start.6 = (bf16[768,128]{1,0:T(8,128)(2,1)}, bf16[768,128]{1,0:T(8,128)(2,1)S(1)}, u32[]{:S(2)}, u32[]{:S(2)}) collective-permute-start(bf16[768,128]{1,0:T(8,128)(2,1)} %get-tuple-element.43), channel_id=1, source_target_pairs={{0,24},{1,28},{2,26},{3,30},{4,25},{5,29},{6,27},{7,31},{8,16},{9,... | collective-permute-start | bytes 589832 | tf_op jit(solution)/shard_map/ppermute | solution.py:295
  11.7 14.5 %collective-permute-start = (bf16[768,128]{1,0:T(8,128)(2,1)}, bf16[768,128]{1,0:T(8,128)(2,1)S(1)}, u32[]{:S(2)}, u32[]{:S(2)}) collective-permute-start(bf16[768,128]{1,0:T(8,128)(2,1)} %get-tuple-element.27), channel_id=1, source_target_pairs={{0,0},{1,4},{2,2},{3,6},{4,1},{5,5},{6,3},{7,7},{8,8},{9,12},{10,1... | collective-permute-start | bytes 589832 | tf_op jit(solution)/shard_map/ppermute | solution.py:295
  13.3 13.4 %collective-permute-start.2 = (bf16[768,128]{1,0:T(8,128)(2,1)}, bf16[768,128]{1,0:T(8,128)(2,1)S(1)}, u32[]{:S(2)}, u32[]{:S(2)}) collective-permute-start(bf16[768,128]{1,0:T(8,128)(2,1)} %get-tuple-element.41), channel_id=1, source_target_pairs={{0,8},{1,12},{2,10},{3,14},{4,9},{5,13},{6,11},{7,15},{8,0},{9,4},... | collective-permute-start | bytes 589832 | tf_op jit(solution)/shard_map/ppermute | solution.py:295
  21.0 7.5 %collective-permute-start.5 = (bf16[768,128]{1,0:T(8,128)(2,1)S(1)}, bf16[768,128]{1,0:T(8,128)(2,1)S(1)}, u32[]{:S(2)}, u32[]{:S(2)}) collective-permute-start(bf16[768,128]{1,0:T(8,128)(2,1)S(1)} %collective-permute-done.4.rest_4_), channel_id=1, source_target_pairs={{0,1},{1,0},{2,3},{3,2},{4,5},{5,4},{6,7},{7,6},{8,9},{9,8},{10,11... | collective-permute-start | bytes 589832 | tf_op jit(solution)/shard_map/ppermute | solution.py:301
  22.5 6.6 %collective-permute-start.7 = (bf16[768,128]{1,0:T(8,128)(2,1)S(1)}, bf16[768,128]{1,0:T(8,128)(2,1)S(1)}, u32[]{:S(2)}, u32[]{:S(2)}) collective-permute-start(bf16[768,128]{1,0:T(8,128)(2,1)S(1)} %collective-permute-done.6.rest_6_), channel_id=1, source_target_pairs={{0,1},{1,0},{2,3},{3,2},{4,5},{5,4},{6,7},{7,6},{8,9},{9,8},{10,11... | collective-permute-start | bytes 589832 | tf_op jit(solution)/shard_map/ppermute | solution.py:301
  26.2 2.9 %collective-permute-start.1 = (bf16[768,128]{1,0:T(8,128)(2,1)S(1)}, bf16[768,128]{1,0:T(8,128)(2,1)S(1)}, u32[]{:S(2)}, u32[]{:S(2)}) collective-permute-start(bf16[768,128]{1,0:T(8,128)(2,1)S(1)} %collective-permute-done.rest_0_), channel_id=1, source_target_pairs={{0,1},{1,0},{2,3},{3,2},{4,5},{5,4},{6,7},{7,6},{8,9},{9,8},{10,11... | collective-permute-start | bytes 589832 | tf_op jit(solution)/shard_map/ppermute | solution.py:301
  26.7 2.3 %collective-permute-start.3 = (bf16[768,128]{1,0:T(8,128)(2,1)S(1)}, bf16[768,128]{1,0:T(8,128)(2,1)S(1)}, u32[]{:S(2)}, u32[]{:S(2)}) collective-permute-start(bf16[768,128]{1,0:T(8,128)(2,1)S(1)} %collective-permute-done.2.rest_2_), channel_id=1, source_target_pairs={{0,1},{1,0},{2,3},{3,2},{4,5},{5,4},{6,7},{7,6},{8,9},{9,8},{10,11... | collective-permute-start | bytes 589832 | tf_op jit(solution)/shard_map/ppermute | solution.py:301
  26.8 2.3 %copy-start.2 = (s32[172]{0:T(256)S(1)}, s32[172]{0:T(256)}, u32[]{:S(2)}) copy-start(s32[172]{0:T(256)} %get-tuple-element.35.where) | copy-start | bytes 2068
  26.8 2.3 %copy-start.3 = (s32[172]{0:T(256)S(1)}, s32[172]{0:T(256)}, u32[]{:S(2)}) copy-start(s32[172]{0:T(256)} %get-tuple-element.37.valid) | copy-start | bytes 2068
  26.8 2.3 %copy-start.4 = (s32[172]{0:T(256)S(1)}, s32[172]{0:T(256)}, u32[]{:S(2)}) copy-start(s32[172]{0:T(256)} %get-tuple-element.38.first) | copy-start | bytes 2068
  26.9 2.2 %copy-start = (s32[576]{0:T(1024)S(1)}, s32[576]{0:T(1024)}, u32[]{:S(2)}) copy-start(s32[576]{0:T(1024)} %get-tuple-element.36.which) | copy-start | bytes 6916
  26.9 13.2 %collective-permute-start.26 = (bf16[256,256]{1,0:T(8,128)(2,1)S(1)}, bf16[256,256]{1,0:T(8,128)(2,1)S(1)}, u32[]{:S(2)}, u32[]{:S(2)}) collective-permute-start(bf16[256,256]{1,0:T(8,128)(2,1)S(1)} %get-tuple-element.49), channel_id=1, source_target_pairs={{0,3},{1,2},{2,1},{3,0},{4,7},{5,6},{6,5},{7,4},{8,11},{9,10},{10,... | collective-permute-start | bytes 393224 | tf_op jit(solution)/shard_map/ppermute | solution.py:304
  28.5 0.7 %copy-start.1 = (s32[172]{0:T(256)S(1)}, s32[172]{0:T(256)}, u32[]{:S(2)}) copy-start(s32[172]{0:T(256)} %get-tuple-element.34.who) | copy-start | bytes 2068
  28.5 13.5 %collective-permute-start.25 = (bf16[256,256]{1,0:T(8,128)(2,1)S(1)}, bf16[256,256]{1,0:T(8,128)(2,1)S(1)}, u32[]{:S(2)}, u32[]{:S(2)}) collective-permute-start(bf16[256,256]{1,0:T(8,128)(2,1)S(1)} %get-tuple-element.50), channel_id=1, source_target_pairs={{0,2},{1,3},{2,0},{3,1},{4,6},{5,7},{6,4},{7,5},{8,10},{9,11},{10,... | collective-permute-start | bytes 393224 | tf_op jit(solution)/shard_map/ppermute | solution.py:304
  29.1 15.8 %collective-permute-start.24 = (bf16[256,256]{1,0:T(8,128)(2,1)S(1)}, bf16[256,256]{1,0:T(8,128)(2,1)S(1)}, u32[]{:S(2)}, u32[]{:S(2)}) collective-permute-start(bf16[256,256]{1,0:T(8,128)(2,1)S(1)} %get-tuple-element.51), channel_id=1, source_target_pairs={{0,1},{1,0},{2,3},{3,2},{4,5},{5,4},{6,7},{7,6},{8,9},{9,8},{10,11... | collective-permute-start | bytes 393224 | tf_op jit(solution)/shard_map/ppermute | solution.py:304
  34.9 8.6 %collective-permute-start.8 = (bf16[256,128]{1,0:T(8,128)(2,1)S(1)}, bf16[256,128]{1,0:T(8,128)(2,1)S(1)}, u32[]{:S(2)}, u32[]{:S(2)}) collective-permute-start(bf16[256,128]{1,0:T(8,128)(2,1)S(1)} %get-tuple-element.44), channel_id=1, source_target_pairs={{0,0},{1,4},{2,2},{3,6},{4,1},{5,5},{6,3},{7,7},{8,8},{9,12},{10,1... | collective-permute-start | bytes 196616 | tf_op jit(solution)/shard_map/ppermute | solution.py:295
  35.5 12.5 %collective-permute-start.9 = (bf16[256,128]{1,0:T(8,128)(2,1)S(1)}, bf16[256,128]{1,0:T(8,128)(2,1)S(1)}, u32[]{:S(2)}, u32[]{:S(2)}) collective-permute-start(bf16[256,128]{1,0:T(8,128)(2,1)S(1)} %get-tuple-element.45), channel_id=1, source_target_pairs={{0,8},{1,12},{2,10},{3,14},{4,9},{5,13},{6,11},{7,15},{8,0},{9,4},... | collective-permute-start | bytes 196616 | tf_op jit(solution)/shard_map/ppermute | solution.py:295
  40.1 8.6 %collective-permute-start.10 = (bf16[256,128]{1,0:T(8,128)(2,1)S(1)}, bf16[256,128]{1,0:T(8,128)(2,1)S(1)}, u32[]{:S(2)}, u32[]{:S(2)}) collective-permute-start(bf16[256,128]{1,0:T(8,128)(2,1)S(1)} %get-tuple-element.46), channel_id=1, source_target_pairs={{0,16},{1,20},{2,18},{3,22},{4,17},{5,21},{6,19},{7,23},{8,24},{9,... | collective-permute-start | bytes 196616 | tf_op jit(solution)/shard_map/ppermute | solution.py:295
  42.0 6.9 %collective-permute-start.11 = (bf16[256,128]{1,0:T(8,128)(2,1)S(1)}, bf16[256,128]{1,0:T(8,128)(2,1)S(1)}, u32[]{:S(2)}, u32[]{:S(2)}) collective-permute-start(bf16[256,128]{1,0:T(8,128)(2,1)S(1)} %get-tuple-element.47), channel_id=1, source_target_pairs={{0,24},{1,28},{2,26},{3,30},{4,25},{5,29},{6,27},{7,31},{8,16},{9,... | collective-permute-start | bytes 196616 | tf_op jit(solution)/shard_map/ppermute | solution.py:295
  43.4 6.9 %collective-permute-start.16 = (bf16[256,128]{1,0:T(8,128)(2,1)S(1)}, bf16[256,128]{1,0:T(8,128)(2,1)S(1)}, u32[]{:S(2)}, u32[]{:S(2)}) collective-permute-start(bf16[256,128]{1,0:T(8,128)(2,1)S(1)} %collective-permute-done.8.refs_0_), channel_id=1, source_target_pairs={{0,2},{1,3},{2,0},{3,1},{4,6},{5,7},{6,4},{7,5},{8,10},{9,11},{10,... | collective-permute-start | bytes 196616 | tf_op jit(solution)/shard_map/ppermute | solution.py:304
  44.9 7.3 %collective-permute-start.12 = (bf16[256,128]{1,0:T(8,128)(2,1)S(1)}, bf16[256,128]{1,0:T(8,128)(2,1)S(1)}, u32[]{:S(2)}, u32[]{:S(2)}) collective-permute-start(bf16[256,128]{1,0:T(8,128)(2,1)S(1)} %collective-permute-done.8.refs_0_), channel_id=1, source_target_pairs={{0,1},{1,0},{2,3},{3,2},{4,5},{5,4},{6,7},{7,6},{8,9},{9,8},{10,11... | collective-permute-start | bytes 196616 | tf_op jit(solution)/shard_map/ppermute | solution.py:304
  48.1 4.6 %collective-permute-start.17 = (bf16[256,128]{1,0:T(8,128)(2,1)S(1)}, bf16[256,128]{1,0:T(8,128)(2,1)S(1)}, u32[]{:S(2)}, u32[]{:S(2)}) collective-permute-start(bf16[256,128]{1,0:T(8,128)(2,1)S(1)} %collective-permute-done.9.refs_1_), channel_id=1, source_target_pairs={{0,2},{1,3},{2,0},{3,1},{4,6},{5,7},{6,4},{7,5},{8,10},{9,11},{10,... | collective-permute-start | bytes 196616 | tf_op jit(solution)/shard_map/ppermute | solution.py:304
  48.7 4.0 %collective-permute-start.13 = (bf16[256,128]{1,0:T(8,128)(2,1)S(1)}, bf16[256,128]{1,0:T(8,128)(2,1)S(1)}, u32[]{:S(2)}, u32[]{:S(2)}) collective-permute-start(bf16[256,128]{1,0:T(8,128)(2,1)S(1)} %collective-permute-done.9.refs_1_), channel_id=1, source_target_pairs={{0,1},{1,0},{2,3},{3,2},{4,5},{5,4},{6,7},{7,6},{8,9},{9,8},{10,11... | collective-permute-start | bytes 196616 | tf_op jit(solution)/shard_map/ppermute | solution.py:304
  48.9 4.3 %collective-permute-start.18 = (bf16[256,128]{1,0:T(8,128)(2,1)S(1)}, bf16[256,128]{1,0:T(8,128)(2,1)S(1)}, u32[]{:S(2)}, u32[]{:S(2)}) collective-permute-start(bf16[256,128]{1,0:T(8,128)(2,1)S(1)} %collective-permute-done.10.refs_2_), channel_id=1, source_target_pairs={{0,2},{1,3},{2,0},{3,1},{4,6},{5,7},{6,4},{7,5},{8,10},{9,11},{10,... | collective-permute-start | bytes 196616 | tf_op jit(solution)/shard_map/ppermute | solution.py:304
  50.3 3.7 %collective-permute-start.14 = (bf16[256,128]{1,0:T(8,128)(2,1)S(1)}, bf16[256,128]{1,0:T(8,128)(2,1)S(1)}, u32[]{:S(2)}, u32[]{:S(2)}) collective-permute-start(bf16[256,128]{1,0:T(8,128)(2,1)S(1)} %collective-permute-done.10.refs_2_), channel_id=1, source_target_pairs={{0,1},{1,0},{2,3},{3,2},{4,5},{5,4},{6,7},{7,6},{8,9},{9,8},{10,11... | collective-permute-start | bytes 196616 | tf_op jit(solution)/shard_map/ppermute | solution.py:304
  52.1 4.3 %collective-permute-start.19 = (bf16[256,128]{1,0:T(8,128)(2,1)S(1)}, bf16[256,128]{1,0:T(8,128)(2,1)S(1)}, u32[]{:S(2)}, u32[]{:S(2)}) collective-permute-start(bf16[256,128]{1,0:T(8,128)(2,1)S(1)} %collective-permute-done.11.refs_3_), channel_id=1, source_target_pairs={{0,2},{1,3},{2,0},{3,1},{4,6},{5,7},{6,4},{7,5},{8,10},{9,11},{10,... | collective-permute-start | bytes 196616 | tf_op jit(solution)/shard_map/ppermute | solution.py:304
  52.7 3.7 %collective-permute-start.15 = (bf16[256,128]{1,0:T(8,128)(2,1)S(1)}, bf16[256,128]{1,0:T(8,128)(2,1)S(1)}, u32[]{:S(2)}, u32[]{:S(2)}) collective-permute-start(bf16[256,128]{1,0:T(8,128)(2,1)S(1)} %collective-permute-done.11.refs_3_), channel_id=1, source_target_pairs={{0,1},{1,0},{2,3},{3,2},{4,5},{5,4},{6,7},{7,6},{8,9},{9,8},{10,11... | collective-permute-start | bytes 196616 | tf_op jit(solution)/shard_map/ppermute | solution.py:304
  52.7 3.7 %collective-permute-start.20 = (bf16[256,128]{1,0:T(8,128)(2,1)S(1)}, bf16[256,128]{1,0:T(8,128)(2,1)S(1)}, u32[]{:S(2)}, u32[]{:S(2)}) collective-permute-start(bf16[256,128]{1,0:T(8,128)(2,1)S(1)} %collective-permute-done.16.refs_8_), channel_id=1, source_target_pairs={{0,1},{1,0},{2,3},{3,2},{4,5},{5,4},{6,7},{7,6},{8,9},{9,8},{10,11... | collective-permute-start | bytes 196616 | tf_op jit(solution)/shard_map/ppermute | solution.py:304
  53.2 3.2 %collective-permute-start.21 = (bf16[256,128]{1,0:T(8,128)(2,1)S(1)}, bf16[256,128]{1,0:T(8,128)(2,1)S(1)}, u32[]{:S(2)}, u32[]{:S(2)}) collective-permute-start(bf16[256,128]{1,0:T(8,128)(2,1)S(1)} %collective-permute-done.17.refs_9_), channel_id=1, source_target_pairs={{0,1},{1,0},{2,3},{3,2},{4,5},{5,4},{6,7},{7,6},{8,9},{9,8},{10,11... | collective-permute-start | bytes 196616 | tf_op jit(solution)/shard_map/ppermute | solution.py:304
  54.0 2.4 %collective-permute-start.22 = (bf16[256,128]{1,0:T(8,128)(2,1)S(1)}, bf16[256,128]{1,0:T(8,128)(2,1)S(1)}, u32[]{:S(2)}, u32[]{:S(2)}) collective-permute-start(bf16[256,128]{1,0:T(8,128)(2,1)S(1)} %collective-permute-done.18.refs_10_), channel_id=1, source_target_pairs={{0,1},{1,0},{2,3},{3,2},{4,5},{5,4},{6,7},{7,6},{8,9},{9,8},{10,11... | collective-permute-start | bytes 196616 | tf_op jit(solution)/shard_map/ppermute | solution.py:304
  56.4 1.3 %collective-permute-start.23 = (bf16[256,128]{1,0:T(8,128)(2,1)S(1)}, bf16[256,128]{1,0:T(8,128)(2,1)S(1)}, u32[]{:S(2)}, u32[]{:S(2)}) collective-permute-start(bf16[256,128]{1,0:T(8,128)(2,1)S(1)} %collective-permute-done.19.refs_11_), channel_id=1, source_target_pairs={{0,1},{1,0},{2,3},{3,2},{4,5},{5,4},{6,7},{7,6},{8,9},{9,8},{10,11... | collective-permute-start | bytes 196616 | tf_op jit(solution)/shard_map/ppermute | solution.py:304
